TPU v7x, 32 devices: a whole 2x2x4 slice. The times are simulated.
32 devices in a mesh: scen: 2 (over x), hour: 4 (over z), reg: 4 (over y, core).
Axes of the slice: x: 2, y: 2, z: 4, core: 2. Of those that a mesh axis runs over, the one named last changes fastest.
Arguments:
- cost_rate: float32 [8, 672, 2048], P('scen', 'hour', 'reg'), may hold values from 0.05 to 1
- invest_cost: float32 [3, 2048], P(None, 'reg'), may hold values from 0.1 to 1
- tile: bfloat16 [4, 256, 2048], P('hour', None, 'reg'), may hold values from -0.1875 to 0.1875
- tile_mask: int32 [4, 256, 2048], P('hour', None, 'reg'), may hold values 0 or 1
- demand: float32 [8, 672, 256], P('scen', 'hour'), may hold values from -6 to 6
- dispatch: float32 [8, 672, 2048], P('scen', 'hour', 'reg'), may hold values from 0 to 1
- dual: float32 [8, 672, 256], P('scen', 'hour'), may hold values from 0 to 1
- cap_dual: float32 [8, 672, 2048], P('scen', 'hour', 'reg'), may hold values from 0 to 1
- capacity: float32 [8, 3, 2048], P('scen', None, 'reg'), may hold values from 0 to 2
- multiplier: float32 [8, 3, 2048], P('scen', None, 'reg'), may hold values from -3 to 3
- consensus: float32 [8, 3, 2048], P('scen', None, 'reg'), may hold values from 0 to 2
- scen_weight: float32 [8], P('scen'), may hold values from 0.1 to 1
- node_of: int32 [3, 8], P(None, 'scen'), may hold values from 0 to 3, as said below
Outputs:
- dispatch_out: float32 [8, 672, 2048], P('scen', 'hour', 'reg')
- dual_out: float32 [8, 672, 256], P('scen', 'hour', 'reg')
- capacity_out: float32 [8, 3, 2048], P('scen', None, 'reg')
- multiplier_out: float32 [8, 3, 2048], P('scen', None, 'reg')
Inputs may be any that keep to these rules, and one draw needn't show every extreme that they name: `node_of`: at each section the nodes are runs of consecutive scenarios, numbered in order from 0; each node of a section lies within one node of the section before; section 0 is one node, the last section has 4 nodes, and node counts grow from section to section.
All inputs are finite; a program needn't handle non-finite values. No bound on the sum of `tile_mask` on one device may be relied on, other than what follows from the above.
Results may differ from a plain program's by a relative error of at most 0.0015.
Values may be sent and summed in bfloat16 or wider, within the bound.
No kernel may reach another device: no remote copies, remote signals or barrier semaphores. Data moves between devices by JAX's collectives and lax.ppermute only.
A program may use at most 64 MiB of HBM per device.

v0:
```python
import jax
import jax.numpy as jnp
from jax import lax
from jax.sharding import PartitionSpec as P

ITERS = 8
RAMP_WEIGHT = 0.5
PENALTY = 1.0
STEP_PRIMAL = 0.3
STEP_INVEST = 0.5
STEP_DUAL = 0.3
STEP_CAP = 0.05


def with_halo(cells, sides, width):
    for axis, dim in sides:
        count = lax.axis_size(axis)
        ends = count - 1
        head = lax.slice_in_dim(cells, 0, width, axis=dim)
        tail = lax.slice_in_dim(cells, cells.shape[dim] - width, cells.shape[dim], axis=dim)
        cells = jnp.concatenate(
            [
                lax.ppermute(tail, axis, [(i, (i + 1) % count) for i in range(ends)]),
                cells,
                lax.ppermute(head, axis, [((i + 1) % count, i) for i in range(ends)]),
            ],
            axis=dim,
        )
    return cells


def safe_average(node_sum, node_mass):
    safe_mass = node_mass + (node_mass <= 0.0).astype(jnp.float32)
    return node_sum / safe_mass[:, :, None]


def shards(
    cost_rate,
    invest_cost,
    tile,
    tile_mask,
    demand,
    dispatch,
    dual,
    cap_dual,
    capacity,
    multiplier,
    consensus,
    scen_weight,
    node_of,
):
    matrix = tile[0] * tile_mask[0].astype(jnp.bfloat16)
    hours_all = dispatch.shape[1] * lax.axis_size("hour")
    reg_count = lax.axis_size("reg")
    reg_place = lax.axis_index("reg")
    cons_part = dual.shape[2] // reg_count
    first_row = reg_place * cons_part
    primal = dispatch
    cap_var = cap_dual
    invest = capacity
    dual_low = dual.astype(jnp.bfloat16)
    dual_var = lax.dynamic_slice_in_dim(dual, first_row, cons_part, 2)
    demand_use = lax.dynamic_slice_in_dim(demand, first_row, cons_part, 2)
    for step_index in range(ITERS):
        padded = with_halo(primal, (("hour", 1),), 1)
        rough = 2.0 * primal - padded[:, :-2] - padded[:, 2:]
        pulled = jnp.einsum("shr,rc->shc", dual_low, matrix, preferred_element_type=jnp.float32)
        grad_x = cost_rate + RAMP_WEIGHT * rough - pulled + cap_var
        zmean = lax.psum(jnp.sum(cap_var, axis=1), "hour") / hours_all
        grad_u = invest_cost[None] + multiplier + PENALTY * (invest - consensus) - zmean[:, None, :]
        primal_new = jnp.maximum(primal - STEP_PRIMAL * grad_x, 0.0)
        invest_new = jnp.maximum(invest - STEP_INVEST * grad_u, 0.0)
        primal_ext = 2.0 * primal_new - primal
        invest_ext = 2.0 * invest_new - invest
        partial_rows = jnp.einsum(
            "shc,rc->shr",
            primal_ext.astype(jnp.bfloat16),
            matrix,
            preferred_element_type=jnp.float32,
        )
        image = lax.psum_scatter(partial_rows, "reg", scatter_dimension=2, tiled=True)
        dual_var = jnp.maximum(dual_var + STEP_DUAL * (demand_use - image), 0.0)
        if step_index + 1 < ITERS:
            dual_low = lax.all_gather(dual_var.astype(jnp.bfloat16), "reg", axis=2, tiled=True)
        cap_var = jnp.maximum(
            cap_var + STEP_CAP * (primal_ext - jnp.sum(invest_ext, axis=1)[:, None, :]), 0.0
        )
        primal = primal_new
        invest = invest_new
    node_count = node_of.shape[1] * lax.axis_size("scen") // 2
    node_ids = jnp.arange(node_count, dtype=jnp.int32)
    one_hot = (node_of[:, :, None] == node_ids[None, None, :]).astype(jnp.float32)
    weighted = scen_weight[:, None, None] * invest
    node_sum = jnp.einsum("gsn,sgc->gnc", one_hot, weighted, precision=lax.Precision.HIGHEST)
    node_mass = jnp.einsum("gsn,s->gn", one_hot, scen_weight, precision=lax.Precision.HIGHEST)
    sum_total, mass_total = lax.psum((node_sum, node_mass), "scen")
    average = safe_average(sum_total, mass_total)
    spread_back = jnp.einsum("gsn,gnc->sgc", one_hot, average, precision=lax.Precision.HIGHEST)
    multiplier_out = multiplier + PENALTY * (invest - spread_back)
    return (primal, dual_var, invest, multiplier_out)


def solution(mesh):
    placed = (
        P("scen", "hour", "reg"),
        P(None, "reg"),
        P("hour", None, "reg"),
        P("hour", None, "reg"),
        P("scen", "hour", None),
        P("scen", "hour", "reg"),
        P("scen", "hour", None),
        P("scen", "hour", "reg"),
        P("scen", None, "reg"),
        P("scen", None, "reg"),
        P("scen", None, "reg"),
        P("scen"),
        P(None, "scen"),
    )
    return jax.shard_map(
        shards,
        mesh=mesh,
        in_specs=placed,
        out_specs=(
            P("scen", "hour", "reg"),
            P("scen", "hour", "reg"),
            P("scen", None, "reg"),
            P("scen", None, "reg"),
        ),
        check_vma=False,
    )
```

profile of v0, /device:TPU:0, one launch (start us, length us, event | category | flops | bytes accessed | tf_op | source)
XLA Modules:
  0.0 344.3 jit_solution(13150075542989649014)
XLA Ops:
  8.3 5.0 %collective-permute-start = (f32[4,1,512]{2,1,0:T(1,128)S(1)}, f32[4,1,512]{2,1,0:T(1,128)S(1)}, u32[]{:S(2)}, u32[]{:S(2)}) collective-permute-start(f32[4,1,512]{2,1,0:T(1,128)S(1)} %get-tuple-element.40), channel_id=1, source_target_pairs={{0,4},{4,8},{8,12},{1,5},{5,9},{9,13},{2,6},{6,10},{10,14},{3,7},{... | collective-permute-start | bytes 24584 | tf_op jit(solution)/shard_map/ppermute | solution.py:23
  13.3 1.3 collective-permute-start.1
  14.6 1.5 reduce_sum.135
  16.1 13.2 %psum.70 = f32[4,512]{1,0:T(4,128)S(1)} all-reduce(f32[4,512]{1,0:T(4,128)S(1)} %reduce_sum.135), channel_id=1, replica_groups=mesh['scen'=2,'hour'=4,'reg'=4] {'hour'}, use_global_device_ids=true, to_apply=%region_2.0 | all-reduce | flops 2048 | bytes 16384 | tf_op jit(solution)/shard_map/psum | solution.py:69
  29.4 5.6 %fusion.161 = (f32[4,512]{1,0:T(4,128)S(1)}, f32[4,168,512]{2,1,0:T(8,128)}, f32[4,168,512]{2,1,0:T(8,128)S(1)}) fusion(f32[4,168,512]{2,1,0:T(8,128)} %param.20, f32[4,512]{1,0:T(4,128)S(1)} %get-tuple-element.24, f32[4,168,512]{2,1,0:T(8,128)} %param.18, f32[4,168,256]{2,1,0:T(8,128)S(1)} %copy-done.19, ...), kind=kOutput, calls=%fused_computation.216 | convolution fusion | flops 182867968 | bytes 7864320 | tf_op jit(solution)/shard_map/shr,rc->shc/dot_general | solution.py:67
  35.1 1.5 fusion.87
  37.0 1.1 constant_dynamic-slice_fusion.1
  38.4 1.3 collective-permute-start.2
  39.7 1.3 collective-permute-start.3
  41.0 11.5 %psum.71 = f32[4,512]{1,0:T(4,128)S(1)} all-reduce(f32[4,512]{1,0:T(4,128)S(1)} %get-tuple-element.22), channel_id=1, replica_groups=mesh['scen'=2,'hour'=4,'reg'=4] {'hour'}, use_global_device_ids=true, to_apply=%region_6.0 | all-reduce | flops 2048 | bytes 16384 | tf_op jit(solution)/shard_map/psum | solution.py:69
  52.5 7.2 %reduce-scatter.9.cloned.1.call-done = f32[4,168,64]{1,2,0:T(8,128)} async-done(((f32[4,168,256]{1,2,0:T(8,128)}), f32[4,168,64]{1,2,0:T(8,128)}) %reduce-scatter.9.cloned.1.call-update) | async-done | bytes 172048 | tf_op jit(solution)/shard_map/reduce_scatter | solution.py:81
  59.8 1.1 fusion.131
  60.9 6.6 %all_gather.21 = bf16[4,168,256]{1,2,0:T(8,128)(2,1)S(1)} all-gather(bf16[4,168,64]{1,2,0:T(8,128)(2,1)S(1)} %fusion.131), channel_id=1, replica_groups=mesh['scen'=2,'hour'=4,'reg'=4] {'reg'}, dimensions={2}, use_global_device_ids=true | all-gather | bytes 430080 | tf_op jit(solution)/shard_map/all_gather | solution.py:84
  67.5 3.6 %fusion.159 = (f32[4,512]{1,0:T(4,128)S(1)}, f32[4,168,512]{2,1,0:T(8,128)}, f32[4,168,512]{2,1,0:T(8,128)S(1)}) fusion(f32[4,168,512]{2,1,0:T(8,128)} %get-tuple-element.23, f32[4,512]{1,0:T(4,128)S(1)} %subtract_reduce_fusion.5, f32[4,168,512]{2,1,0:T(8,128)S(1)} %get-tuple-element.42, bf16[4,168,256]{1,2,0:T(8,128)(2,1)S(1)} %all_gather.21, ...), kind=kOutput, calls=%fused_computation.214 | convolution fusion | flops 182695936 | bytes 7520256 | tf_op jit(solution)/shard_map/shr,rc->shc/dot_general | solution.py:67
  71.1 1.1 copy-done.1
  72.2 1.5 fusion.85
  74.7 3.4 collective-permute-start.4
  78.1 1.3 collective-permute-start.5
  79.4 13.1 %psum.72 = f32[4,512]{1,0:T(4,128)S(1)} all-reduce(f32[4,512]{1,0:T(4,128)S(1)} %get-tuple-element.18), channel_id=1, replica_groups=mesh['scen'=2,'hour'=4,'reg'=4] {'hour'}, use_global_device_ids=true, to_apply=%region_10.0 | all-reduce | flops 2048 | bytes 16384 | tf_op jit(solution)/shard_map/psum | solution.py:69
  92.6 6.6 %reduce-scatter.11.cloned.1.call-done = f32[4,168,64]{1,2,0:T(8,128)} async-done(((f32[4,168,256]{1,2,0:T(8,128)}), f32[4,168,64]{1,2,0:T(8,128)}) %reduce-scatter.11.cloned.1.call-update) | async-done | bytes 172048 | tf_op jit(solution)/shard_map/reduce_scatter | solution.py:81
  100.2 6.6 %all_gather.22 = bf16[4,168,256]{1,2,0:T(8,128)(2,1)S(1)} all-gather(bf16[4,168,64]{1,2,0:T(8,128)(2,1)S(1)} %get-tuple-element.20), channel_id=1, replica_groups=mesh['scen'=2,'hour'=4,'reg'=4] {'reg'}, dimensions={2}, use_global_device_ids=true | all-gather | bytes 430080 | tf_op jit(solution)/shard_map/all_gather | solution.py:84
  106.8 4.0 %fusion.158 = (f32[4,512]{1,0:T(4,128)S(1)}, f32[4,168,512]{2,1,0:T(8,128)}, f32[4,168,512]{2,1,0:T(8,128)S(1)}) fusion(f32[4,168,512]{2,1,0:T(8,128)} %get-tuple-element.19, f32[4,512]{1,0:T(4,128)S(1)} %subtract_reduce_fusion.4, f32[4,168,512]{2,1,0:T(8,128)S(1)} %copy-done.2, bf16[4,168,256]{1,2,0:T(8,128)(2,1)S(1)} %all_gather.22, ...), kind=kOutput, calls=%fused_computation.213 | convolution fusion | flops 182695936 | bytes 7520256 | tf_op jit(solution)/shard_map/shr,rc->shc/dot_general | solution.py:67
  111.9 1.5 fusion.83
  114.4 3.4 collective-permute-start.6
  117.8 1.3 collective-permute-start.7
  119.1 13.1 %psum.73 = f32[4,512]{1,0:T(4,128)S(1)} all-reduce(f32[4,512]{1,0:T(4,128)S(1)} %get-tuple-element.16), channel_id=1, replica_groups=mesh['scen'=2,'hour'=4,'reg'=4] {'hour'}, use_global_device_ids=true, to_apply=%region_14.0 | all-reduce | flops 2048 | bytes 16384 | tf_op jit(solution)/shard_map/psum | solution.py:69
  132.2 6.7 %reduce-scatter.13.cloned.1.call-done = f32[4,168,64]{1,2,0:T(8,128)} async-done(((f32[4,168,256]{1,2,0:T(8,128)}), f32[4,168,64]{1,2,0:T(8,128)}) %reduce-scatter.13.cloned.1.call-update) | async-done | bytes 172048 | tf_op jit(solution)/shard_map/reduce_scatter | solution.py:81
  139.9 6.6 %all_gather.23 = bf16[4,168,256]{1,2,0:T(8,128)(2,1)S(1)} all-gather(bf16[4,168,64]{1,2,0:T(8,128)(2,1)S(1)} %fusion.132), channel_id=1, replica_groups=mesh['scen'=2,'hour'=4,'reg'=4] {'reg'}, dimensions={2}, use_global_device_ids=true | all-gather | bytes 430080 | tf_op jit(solution)/shard_map/all_gather | solution.py:84
  146.5 5.4 %fusion.156 = (f32[4,512]{1,0:T(4,128)S(1)}, f32[4,168,512]{2,1,0:T(8,128)}, f32[4,168,512]{2,1,0:T(8,128)S(1)}) fusion(f32[4,168,512]{2,1,0:T(8,128)} %get-tuple-element.17, f32[4,512]{1,0:T(4,128)S(1)} %subtract_reduce_fusion.3, f32[4,168,512]{2,1,0:T(8,128)} %copy-done.3, bf16[4,168,256]{1,2,0:T(8,128)(2,1)S(1)} %all_gather.23, ...), kind=kOutput, calls=%fused_computation.211 | convolution fusion | flops 182695936 | bytes 7520256 | tf_op jit(solution)/shard_map/shr,rc->shc/dot_general | solution.py:67
  151.9 1.5 fusion.81
  153.5 3.4 collective-permute-start.8
  156.9 1.3 collective-permute-start.9
  158.2 13.6 %psum.74 = f32[4,512]{1,0:T(4,128)S(1)} all-reduce(f32[4,512]{1,0:T(4,128)S(1)} %get-tuple-element.12), channel_id=1, replica_groups=mesh['scen'=2,'hour'=4,'reg'=4] {'hour'}, use_global_device_ids=true, to_apply=%region_18.0 | all-reduce | flops 2048 | bytes 16384 | tf_op jit(solution)/shard_map/psum | solution.py:69
  171.9 7.0 %reduce-scatter.15.cloned.1.call-done = f32[4,168,64]{1,2,0:T(8,128)} async-done(((f32[4,168,256]{1,2,0:T(8,128)}), f32[4,168,64]{1,2,0:T(8,128)}) %reduce-scatter.15.cloned.1.call-update) | async-done | bytes 172048 | tf_op jit(solution)/shard_map/reduce_scatter | solution.py:81
  178.9 1.1 fusion.157
  180.1 6.8 %all_gather.24 = bf16[4,168,256]{1,2,0:T(8,128)(2,1)S(1)} all-gather(bf16[4,168,64]{1,2,0:T(8,128)(2,1)S(1)} %get-tuple-element.14), channel_id=1, replica_groups=mesh['scen'=2,'hour'=4,'reg'=4] {'reg'}, dimensions={2}, use_global_device_ids=true | all-gather | bytes 430080 | tf_op jit(solution)/shard_map/all_gather | solution.py:84
  186.9 3.6 %fusion.155 = (f32[4,512]{1,0:T(4,128)S(1)}, f32[4,168,512]{2,1,0:T(8,128)}, f32[4,168,512]{2,1,0:T(8,128)S(1)}) fusion(f32[4,168,512]{2,1,0:T(8,128)} %get-tuple-element.13, f32[4,512]{1,0:T(4,128)S(1)} %subtract_reduce_fusion.2, f32[4,168,512]{2,1,0:T(8,128)S(1)} %get-tuple-element.45, bf16[4,168,256]{1,2,0:T(8,128)(2,1)S(1)} %all_gather.24, ...), kind=kOutput, calls=%fused_computation.210 | convolution fusion | flops 182695936 | bytes 7520256 | tf_op jit(solution)/shard_map/shr,rc->shc/dot_general | solution.py:67
  191.6 1.5 fusion.79
  194.0 3.4 collective-permute-start.10
  197.4 1.3 collective-permute-start.11
  198.7 13.1 %psum.75 = f32[4,512]{1,0:T(4,128)S(1)} all-reduce(f32[4,512]{1,0:T(4,128)S(1)} %get-tuple-element.10), channel_id=1, replica_groups=mesh['scen'=2,'hour'=4,'reg'=4] {'hour'}, use_global_device_ids=true, to_apply=%region_22.0 | all-reduce | flops 2048 | bytes 16384 | tf_op jit(solution)/shard_map/psum | solution.py:69
  211.9 6.7 %reduce-scatter.17.cloned.1.call-done = f32[4,168,64]{1,2,0:T(8,128)} async-done(((f32[4,168,256]{1,2,0:T(8,128)}), f32[4,168,64]{1,2,0:T(8,128)}) %reduce-scatter.17.cloned.1.call-update) | async-done | bytes 172048 | tf_op jit(solution)/shard_map/reduce_scatter | solution.py:81
  219.6 6.6 %all_gather.25 = bf16[4,168,256]{1,2,0:T(8,128)(2,1)S(1)} all-gather(bf16[4,168,64]{1,2,0:T(8,128)(2,1)S(1)} %fusion.133), channel_id=1, replica_groups=mesh['scen'=2,'hour'=4,'reg'=4] {'reg'}, dimensions={2}, use_global_device_ids=true | all-gather | bytes 430080 | tf_op jit(solution)/shard_map/all_gather | solution.py:84
  226.2 5.4 %fusion.153 = (f32[4,512]{1,0:T(4,128)S(1)}, f32[4,168,512]{2,1,0:T(8,128)}, f32[4,168,512]{2,1,0:T(8,128)S(1)}) fusion(f32[4,168,512]{2,1,0:T(8,128)} %get-tuple-element.11, f32[4,512]{1,0:T(4,128)S(1)} %subtract_reduce_fusion.1, f32[4,168,512]{2,1,0:T(8,128)} %copy-done.5, bf16[4,168,256]{1,2,0:T(8,128)(2,1)S(1)} %all_gather.25, ...), kind=kOutput, calls=%fused_computation.208 | convolution fusion | flops 182695936 | bytes 7520256 | tf_op jit(solution)/shard_map/shr,rc->shc/dot_general | solution.py:67
  231.6 1.5 fusion.77
  233.2 4.0 %collective-permute-start.12 = (f32[4,1,512]{2,1,0:T(1,128)S(1)}, f32[4,1,512]{2,1,0:T(1,128)}, u32[]{:S(2)}, u32[]{:S(2)}) collective-permute-start(f32[4,1,512]{2,1,0:T(1,128)S(1)} %get-tuple-element.28), channel_id=1, source_target_pairs={{0,4},{4,8},{8,12},{1,5},{5,9},{9,13},{2,6},{6,10},{10,14},{3,7},{... | collective-permute-start | bytes 24584 | tf_op jit(solution)/shard_map/ppermute | solution.py:23
  237.1 1.3 collective-permute-start.13
  238.4 13.0 %psum.76 = f32[4,512]{1,0:T(4,128)S(1)} all-reduce(f32[4,512]{1,0:T(4,128)S(1)} %get-tuple-element.6), channel_id=1, replica_groups=mesh['scen'=2,'hour'=4,'reg'=4] {'hour'}, use_global_device_ids=true, to_apply=%region_26.0 | all-reduce | flops 2048 | bytes 16384 | tf_op jit(solution)/shard_map/psum | solution.py:69
  251.6 7.0 %reduce-scatter.19.cloned.1.call-done = f32[4,168,64]{1,2,0:T(8,128)} async-done(((f32[4,168,256]{1,2,0:T(8,128)}), f32[4,168,64]{1,2,0:T(8,128)}) %reduce-scatter.19.cloned.1.call-update) | async-done | bytes 172048 | tf_op jit(solution)/shard_map/reduce_scatter | solution.py:81
  258.6 1.1 fusion.154
  259.7 6.6 %all_gather.26 = bf16[4,168,256]{1,2,0:T(8,128)(2,1)S(1)} all-gather(bf16[4,168,64]{1,2,0:T(8,128)(2,1)S(1)} %get-tuple-element.8), channel_id=1, replica_groups=mesh['scen'=2,'hour'=4,'reg'=4] {'reg'}, dimensions={2}, use_global_device_ids=true | all-gather | bytes 430080 | tf_op jit(solution)/shard_map/all_gather | solution.py:84
  266.4 2.5 fusion.130
  270.0 1.5 fusion.75
  272.5 3.4 collective-permute-start.14
  275.8 1.3 collective-permute-start.15
  277.1 19.9 %reduce-scatter.21.cloned.1.call-done = f32[4,168,64]{1,2,0:T(8,128)} async-done(((f32[4,168,256]{1,2,0:T(8,128)}), f32[4,168,64]{1,2,0:T(8,128)}) %reduce-scatter.21.cloned.1.call-update) | async-done | bytes 172048 | tf_op jit(solution)/shard_map/reduce_scatter | solution.py:81
  297.0 1.1 fusion.134
  298.1 6.6 %all_gather.27 = bf16[4,168,256]{1,2,0:T(8,128)(2,1)S(1)} all-gather(bf16[4,168,64]{1,2,0:T(8,128)(2,1)S(1)} %fusion.134), channel_id=1, replica_groups=mesh['scen'=2,'hour'=4,'reg'=4] {'reg'}, dimensions={2}, use_global_device_ids=true | all-gather | bytes 430080 | tf_op jit(solution)/shard_map/all_gather | solution.py:84
  304.7 2.8 fusion.7
  308.6 1.5 fusion.74
  310.4 11.8 %psum.77 = f32[4,512]{1,0:T(4,128)S(1)} all-reduce(f32[4,512]{1,0:T(4,128)S(1)} %get-tuple-element.48), channel_id=1, replica_groups=mesh['scen'=2,'hour'=4,'reg'=4] {'hour'}, use_global_device_ids=true, to_apply=%region_30.0 | all-reduce | flops 2048 | bytes 16384 | tf_op jit(solution)/shard_map/psum | solution.py:69
  322.7 8.3 %all-reduce = (f32[3,4,512]{2,1,0:T(4,128)S(1)}, f32[3,4]{1,0:T(4,128)S(1)}) all-reduce(f32[3,4,512]{2,1,0:T(4,128)S(1)} %fusion.135, f32[3,4]{1,0:T(4,128)S(1)} %bitcast.85), channel_id=1, replica_groups=mesh['scen'=2,'hour'=4,'reg'=4] {'scen'}, use_global_device_ids=true, to_apply=%region_31.0 | all-reduce | flops 6156 | bytes 49248 | tf_op jit(solution)/shard_map/psum | solution.py:96
  331.8 3.9 %reduce-scatter.23.cloned.1.call-done = f32[4,168,64]{1,2,0:T(8,128)} async-done(((f32[4,168,256]{1,2,0:T(8,128)}), f32[4,168,64]{1,2,0:T(8,128)}) %reduce-scatter.23.cloned.1.call-update) | async-done | bytes 172048 | tf_op jit(solution)/shard_map/reduce_scatter | solution.py:81
  335.7 1.7 add_maximum_fusion.7
  (123 shorter events, 15.3 us)
Async XLA Ops:
  7.2 29.5 %copy-start = (f32[4,168,256]{2,1,0:T(8,128)S(1)}, f32[4,168,256]{2,1,0:T(8,128)}, u32[]{:S(2)}) copy-start(f32[4,168,256]{2,1,0:T(8,128)} %param.17) | copy-start | bytes 2064388
  7.2 22.1 %copy-start.18 = (bf16[1,256,512]{2,1,0:T(8,128)(2,1)S(1)}, bf16[1,256,512]{2,1,0:T(8,128)(2,1)}, u32[]{:S(2)}) copy-start(bf16[1,256,512]{2,1,0:T(8,128)(2,1)} %param.15) | copy-start | bytes 786436
  7.2 22.1 %copy-start.17 = (s32[1,256,512]{2,1,0:T(8,128)S(1)}, s32[1,256,512]{2,1,0:T(8,128)}, u32[]{:S(2)}) copy-start(s32[1,256,512]{2,1,0:T(8,128)} %param.16) | copy-start | bytes 1572868
  7.2 22.1 %copy-start.22 = (f32[3,512]{1,0:T(4,128)S(1)}, f32[3,512]{1,0:T(4,128)}, u32[]{:S(2)}) copy-start(f32[3,512]{1,0:T(4,128)} %param.14) | copy-start | bytes 18436
  7.2 22.1 %copy-start.9 = (f32[4,3,512]{2,0,1:T(4,128)S(1)}, f32[4,3,512]{2,0,1:T(4,128)}, u32[]{:S(2)}) copy-start(f32[4,3,512]{2,0,1:T(4,128)} %param.21) | copy-start | bytes 73732
  7.2 22.1 %copy-start.21 = (f32[4,3,512]{2,0,1:T(4,128)S(1)}, f32[4,3,512]{2,0,1:T(4,128)}, u32[]{:S(2)}) copy-start(f32[4,3,512]{2,0,1:T(4,128)} %param.22) | copy-start | bytes 73732
  7.2 22.1 %copy-start.10 = (f32[4,3,512]{2,0,1:T(4,128)S(1)}, f32[4,3,512]{2,0,1:T(4,128)}, u32[]{:S(2)}) copy-start(f32[4,3,512]{2,0,1:T(4,128)} %param.23) | copy-start | bytes 73732
  7.2 22.2 %copy-start.19 = (f32[4,168,256]{2,1,0:T(8,128)S(1)}, f32[4,168,256]{2,1,0:T(8,128)}, u32[]{:S(2)}) copy-start(f32[4,168,256]{2,1,0:T(8,128)} %param.19) | copy-start | bytes 2064388
  7.3 52.5 %reduce-scatter.9.cloned.1.call-start = ((), (), s32[]{:S(2)}) async-start(), calls=%async_computation.8 | async-start | bytes 1310720 | tf_op jit(solution)/shard_map/reduce_scatter | solution.py:81
  8.3 21.1 %collective-permute-start = (f32[4,1,512]{2,1,0:T(1,128)S(1)}, f32[4,1,512]{2,1,0:T(1,128)S(1)}, u32[]{:S(2)}, u32[]{:S(2)}) collective-permute-start(f32[4,1,512]{2,1,0:T(1,128)S(1)} %get-tuple-element.40), channel_id=1, source_target_pairs={{0,4},{4,8},{8,12},{1,5},{5,9},{9,13},{2,6},{6,10},{10,14},{3,7},{... | collective-permute-start | bytes 24584 | tf_op jit(solution)/shard_map/ppermute | solution.py:23
  13.3 16.1 %collective-permute-start.1 = (f32[4,1,512]{2,1,0:T(1,128)S(1)}, f32[4,1,512]{2,1,0:T(1,128)S(1)}, u32[]{:S(2)}, u32[]{:S(2)}) collective-permute-start(f32[4,1,512]{2,1,0:T(1,128)S(1)} %get-tuple-element.41), channel_id=1, source_target_pairs={{4,0},{8,4},{12,8},{5,1},{9,5},{13,9},{6,2},{10,6},{14,10},{7,3},{... | collective-permute-start | bytes 24584 | tf_op jit(solution)/shard_map/ppermute | solution.py:25
  29.4 5.6 %copy-start.11 = (f32[4,168,512]{2,1,0:T(8,128)S(1)}, f32[4,168,512]{2,1,0:T(8,128)}, u32[]{:S(2)}) copy-start(f32[4,168,512]{2,1,0:T(8,128)} %param.18) | copy-start | bytes 4128772
  36.6 62.6 %reduce-scatter.11.cloned.1.call-start = ((), (), s32[]{:S(2)}) async-start(), calls=%async_computation.9 | async-start | bytes 1310720 | tf_op jit(solution)/shard_map/reduce_scatter | solution.py:81
  38.4 29.1 %collective-permute-start.2 = (f32[4,1,512]{2,1,0:T(1,128)S(1)}, f32[4,1,512]{2,1,0:T(1,128)S(1)}, u32[]{:S(2)}, u32[]{:S(2)}) collective-permute-start(f32[4,1,512]{2,1,0:T(1,128)S(1)} %get-tuple-element.38), channel_id=1, source_target_pairs={{0,4},{4,8},{8,12},{1,5},{5,9},{9,13},{2,6},{6,10},{10,14},{3,7},{... | collective-permute-start | bytes 24584 | tf_op jit(solution)/shard_map/ppermute | solution.py:23
  39.7 27.8 %collective-permute-start.3 = (f32[4,1,512]{2,1,0:T(1,128)S(1)}, f32[4,1,512]{2,1,0:T(1,128)S(1)}, u32[]{:S(2)}, u32[]{:S(2)}) collective-permute-start(f32[4,1,512]{2,1,0:T(1,128)S(1)} %get-tuple-element.39), channel_id=1, source_target_pairs={{4,0},{8,4},{12,8},{5,1},{9,5},{13,9},{6,2},{10,6},{14,10},{7,3},{... | collective-permute-start | bytes 24584 | tf_op jit(solution)/shard_map/ppermute | solution.py:25
  59.8 7.7 %copy-start.23 = (f32[4,168,512]{2,1,0:T(8,128)S(1)}, f32[4,168,512]{2,1,0:T(8,128)}, u32[]{:S(2)}) copy-start(f32[4,168,512]{2,1,0:T(8,128)} %param.13) | copy-start | bytes 4128772
  71.1 1.1 copy-start.1
  73.7 25.5 %copy-start.14 = (f32[4,168,64]{1,2,0:T(8,128)S(1)}, f32[4,168,64]{1,2,0:T(8,128)}, u32[]{:S(2)}) copy-start(f32[4,168,64]{1,2,0:T(8,128)} %reduce-scatter.9.cloned.1.call-done) | copy-start | bytes 516100
  73.7 33.2 %copy-start.2 = (f32[4,168,512]{2,1,0:T(8,128)S(1)}, f32[4,168,512]{2,1,0:T(8,128)}, u32[]{:S(2)}) copy-start(f32[4,168,512]{2,1,0:T(8,128)} %copy-done.1) | copy-start | bytes 4128772
  73.7 65.2 %reduce-scatter.13.cloned.1.call-start = ((), (), s32[]{:S(2)}) async-start(), calls=%async_computation.10 | async-start | bytes 1310720 | tf_op jit(solution)/shard_map/reduce_scatter | solution.py:81
  74.7 32.1 %collective-permute-start.4 = (f32[4,1,512]{2,1,0:T(1,128)S(1)}, f32[4,1,512]{2,1,0:T(1,128)S(1)}, u32[]{:S(2)}, u32[]{:S(2)}) collective-permute-start(f32[4,1,512]{2,1,0:T(1,128)S(1)} %get-tuple-element.36), channel_id=1, source_target_pairs={{0,4},{4,8},{8,12},{1,5},{5,9},{9,13},{2,6},{6,10},{10,14},{3,7},{... | collective-permute-start | bytes 24584 | tf_op jit(solution)/shard_map/ppermute | solution.py:23
  78.1 28.7 %collective-permute-start.5 = (f32[4,1,512]{2,1,0:T(1,128)S(1)}, f32[4,1,512]{2,1,0:T(1,128)S(1)}, u32[]{:S(2)}, u32[]{:S(2)}) collective-permute-start(f32[4,1,512]{2,1,0:T(1,128)S(1)} %get-tuple-element.37), channel_id=1, source_target_pairs={{4,0},{8,4},{12,8},{5,1},{9,5},{13,9},{6,2},{10,6},{14,10},{7,3},{... | collective-permute-start | bytes 24584 | tf_op jit(solution)/shard_map/ppermute | solution.py:25
  110.8 1.1 copy-start.3
  113.4 65.5 %reduce-scatter.15.cloned.1.call-start = ((), (), s32[]{:S(2)}) async-start(), calls=%async_computation.11 | async-start | bytes 1310720 | tf_op jit(solution)/shard_map/reduce_scatter | solution.py:81
  114.4 32.2 %collective-permute-start.6 = (f32[4,1,512]{2,1,0:T(1,128)S(1)}, f32[4,1,512]{2,1,0:T(1,128)S(1)}, u32[]{:S(2)}, u32[]{:S(2)}) collective-permute-start(f32[4,1,512]{2,1,0:T(1,128)S(1)} %get-tuple-element.34), channel_id=1, source_target_pairs={{0,4},{4,8},{8,12},{1,5},{5,9},{9,13},{2,6},{6,10},{10,14},{3,7},{... | collective-permute-start | bytes 24584 | tf_op jit(solution)/shard_map/ppermute | solution.py:23
  117.8 28.8 %collective-permute-start.7 = (f32[4,1,512]{2,1,0:T(1,128)S(1)}, f32[4,1,512]{2,1,0:T(1,128)S(1)}, u32[]{:S(2)}, u32[]{:S(2)}) collective-permute-start(f32[4,1,512]{2,1,0:T(1,128)S(1)} %get-tuple-element.35), channel_id=1, source_target_pairs={{4,0},{8,4},{12,8},{5,1},{9,5},{13,9},{6,2},{10,6},{14,10},{7,3},{... | collective-permute-start | bytes 24584 | tf_op jit(solution)/shard_map/ppermute | solution.py:25
  146.5 5.4 %copy-start.4 = (f32[4,168,512]{2,1,0:T(8,128)S(1)}, f32[4,168,512]{2,1,0:T(8,128)}, u32[]{:S(2)}) copy-start(f32[4,168,512]{2,1,0:T(8,128)} %copy-done.3) | copy-start | bytes 4128772
  153.4 25.5 %copy-start.15 = (f32[4,168,64]{1,2,0:T(8,128)S(1)}, f32[4,168,64]{1,2,0:T(8,128)}, u32[]{:S(2)}) copy-start(f32[4,168,64]{1,2,0:T(8,128)} %reduce-scatter.13.cloned.1.call-done) | copy-start | bytes 516100
  153.4 65.1 %reduce-scatter.17.cloned.1.call-start = ((), (), s32[]{:S(2)}) async-start(), calls=%async_computation.12 | async-start | bytes 1310720 | tf_op jit(solution)/shard_map/reduce_scatter | solution.py:81
  153.5 33.4 %collective-permute-start.8 = (f32[4,1,512]{2,1,0:T(1,128)S(1)}, f32[4,1,512]{2,1,0:T(1,128)S(1)}, u32[]{:S(2)}, u32[]{:S(2)}) collective-permute-start(f32[4,1,512]{2,1,0:T(1,128)S(1)} %get-tuple-element.32), channel_id=1, source_target_pairs={{0,4},{4,8},{8,12},{1,5},{5,9},{9,13},{2,6},{6,10},{10,14},{3,7},{... | collective-permute-start | bytes 24584 | tf_op jit(solution)/shard_map/ppermute | solution.py:23
  156.9 30.0 %collective-permute-start.9 = (f32[4,1,512]{2,1,0:T(1,128)S(1)}, f32[4,1,512]{2,1,0:T(1,128)}, u32[]{:S(2)}, u32[]{:S(2)}) collective-permute-start(f32[4,1,512]{2,1,0:T(1,128)S(1)} %get-tuple-element.33), channel_id=1, source_target_pairs={{4,0},{8,4},{12,8},{5,1},{9,5},{13,9},{6,2},{10,6},{14,10},{7,3},{... | collective-permute-start | bytes 24584 | tf_op jit(solution)/shard_map/ppermute | solution.py:25
  178.9 7.9 %copy-start.24 = (f32[4,168,512]{2,1,0:T(8,128)S(1)}, f32[4,168,512]{2,1,0:T(8,128)}, u32[]{:S(2)}) copy-start(f32[4,168,512]{2,1,0:T(8,128)} %param.13) | copy-start | bytes 4128772
  190.5 1.1 copy-start.5
  193.1 65.5 %reduce-scatter.19.cloned.1.call-start = ((), (), s32[]{:S(2)}) async-start(), calls=%async_computation.13 | async-start | bytes 1310720 | tf_op jit(solution)/shard_map/reduce_scatter | solution.py:81
  194.0 32.2 %collective-permute-start.10 = (f32[4,1,512]{2,1,0:T(1,128)S(1)}, f32[4,1,512]{2,1,0:T(1,128)S(1)}, u32[]{:S(2)}, u32[]{:S(2)}) collective-permute-start(f32[4,1,512]{2,1,0:T(1,128)S(1)} %get-tuple-element.30), channel_id=1, source_target_pairs={{0,4},{4,8},{8,12},{1,5},{5,9},{9,13},{2,6},{6,10},{10,14},{3,7},{... | collective-permute-start | bytes 24584 | tf_op jit(solution)/shard_map/ppermute | solution.py:23
  197.4 28.8 %collective-permute-start.11 = (f32[4,1,512]{2,1,0:T(1,128)S(1)}, f32[4,1,512]{2,1,0:T(1,128)S(1)}, u32[]{:S(2)}, u32[]{:S(2)}) collective-permute-start(f32[4,1,512]{2,1,0:T(1,128)S(1)} %get-tuple-element.31), channel_id=1, source_target_pairs={{4,0},{8,4},{12,8},{5,1},{9,5},{13,9},{6,2},{10,6},{14,10},{7,3},{... | collective-permute-start | bytes 24584 | tf_op jit(solution)/shard_map/ppermute | solution.py:25
  226.2 5.4 %copy-start.6 = (f32[4,168,512]{2,1,0:T(8,128)S(1)}, f32[4,168,512]{2,1,0:T(8,128)}, u32[]{:S(2)}) copy-start(f32[4,168,512]{2,1,0:T(8,128)} %copy-done.5) | copy-start | bytes 4128772
  233.1 25.5 %copy-start.16 = (f32[4,168,64]{1,2,0:T(8,128)S(1)}, f32[4,168,64]{1,2,0:T(8,128)}, u32[]{:S(2)}) copy-start(f32[4,168,64]{1,2,0:T(8,128)} %reduce-scatter.17.cloned.1.call-done) | copy-start | bytes 516100
  233.1 63.9 %reduce-scatter.21.cloned.1.call-start = ((), (), s32[]{:S(2)}) async-start(), calls=%async_computation.14 | async-start | bytes 1310720 | tf_op jit(solution)/shard_map/reduce_scatter | solution.py:81
  233.2 33.2 %collective-permute-start.12 = (f32[4,1,512]{2,1,0:T(1,128)S(1)}, f32[4,1,512]{2,1,0:T(1,128)}, u32[]{:S(2)}, u32[]{:S(2)}) collective-permute-start(f32[4,1,512]{2,1,0:T(1,128)S(1)} %get-tuple-element.28), channel_id=1, source_target_pairs={{0,4},{4,8},{8,12},{1,5},{5,9},{9,13},{2,6},{6,10},{10,14},{3,7},{... | collective-permute-start | bytes 24584 | tf_op jit(solution)/shard_map/ppermute | solution.py:23
  237.1 29.2 %collective-permute-start.13 = (f32[4,1,512]{2,1,0:T(1,128)S(1)}, f32[4,1,512]{2,1,0:T(1,128)}, u32[]{:S(2)}, u32[]{:S(2)}) collective-permute-start(f32[4,1,512]{2,1,0:T(1,128)S(1)} %get-tuple-element.29), channel_id=1, source_target_pairs={{4,0},{8,4},{12,8},{5,1},{9,5},{13,9},{6,2},{10,6},{14,10},{7,3},{... | collective-permute-start | bytes 24584 | tf_op jit(solution)/shard_map/ppermute | solution.py:25
  258.6 7.8 %copy-start.25 = (f32[4,168,512]{2,1,0:T(8,128)S(1)}, f32[4,168,512]{2,1,0:T(8,128)}, u32[]{:S(2)}) copy-start(f32[4,168,512]{2,1,0:T(8,128)} %param.13) | copy-start | bytes 4128772
  268.9 1.1 copy-start.7
  271.5 64.2 %reduce-scatter.23.cloned.1.call-start = ((), (), s32[]{:S(2)}) async-start(), calls=%async_computation.15 | async-start | bytes 1310720 | tf_op jit(solution)/shard_map/reduce_scatter | solution.py:81
  272.5 32.3 %collective-permute-start.14 = (f32[4,1,512]{2,1,0:T(1,128)S(1)}, f32[4,1,512]{2,1,0:T(1,128)S(1)}, u32[]{:S(2)}, u32[]{:S(2)}) collective-permute-start(f32[4,1,512]{2,1,0:T(1,128)S(1)} %get-tuple-element.26), channel_id=1, source_target_pairs={{0,4},{4,8},{8,12},{1,5},{5,9},{9,13},{2,6},{6,10},{10,14},{3,7},{... | collective-permute-start | bytes 24584 | tf_op jit(solution)/shard_map/ppermute | solution.py:23
  275.8 28.9 %collective-permute-start.15 = (f32[4,1,512]{2,1,0:T(1,128)S(1)}, f32[4,1,512]{2,1,0:T(1,128)S(1)}, u32[]{:S(2)}, u32[]{:S(2)}) collective-permute-start(f32[4,1,512]{2,1,0:T(1,128)S(1)} %get-tuple-element.27), channel_id=1, source_target_pairs={{4,0},{8,4},{12,8},{5,1},{9,5},{13,9},{6,2},{10,6},{14,10},{7,3},{... | collective-permute-start | bytes 24584 | tf_op jit(solution)/shard_map/ppermute | solution.py:25
  297.0 7.7 %copy-start.8 = (f32[4,168,512]{2,1,0:T(8,128)S(1)}, f32[4,168,512]{2,1,0:T(8,128)}, u32[]{:S(2)}) copy-start(f32[4,168,512]{2,1,0:T(8,128)} %copy-done.7) | copy-start | bytes 4128772
  307.6 1.1 copy-start.12
  308.6 1.5 copy-start.26
  308.6 1.5 copy-start.27
  310.1 25.6 %copy-start.13 = (f32[4,168,64]{1,2,0:T(8,128)S(1)}, f32[4,168,64]{1,2,0:T(8,128)}, u32[]{:S(2)}) copy-start(f32[4,168,64]{1,2,0:T(8,128)} %reduce-scatter.21.cloned.1.call-done) | copy-start | bytes 516100
  322.4 15.1 %copy-start.20 = (f32[4,3,512]{2,0,1:T(4,128)}, f32[4,3,512]{2,0,1:T(4,128)S(1)}, u32[]{:S(2)}) copy-start(f32[4,3,512]{2,0,1:T(4,128)S(1)} %subtract_maximum_fusion) | copy-start | bytes 73732
Sparse Core Ops, SparseCore 0:
  36.7 23.0 reduce-scatter.8
  73.8 25.3 reduce-scatter.10
  113.6 25.3 reduce-scatter.12
  153.6 25.3 reduce-scatter.14
  193.2 25.3 reduce-scatter.16
  233.2 25.3 reduce-scatter.18
  271.6 25.3 reduce-scatter.20
  310.3 25.3 reduce-scatter.22
where the time goes:
time: 346 us; the launch traced here: 344 us
  blocking collectives  157 us (45%)
  waiting for transfers between devices  65.1 us (19%)
  matrix products  46.1 us (13%)
  starting transfers between devices  37.8 us (11%)
  between operations  14.8 us (4%)
  local copies, waits for them, and re-layouts  11.9 us (3%)
  other arithmetic  11.5 us (3%)
    psum x8, blocking collectives, shards(): zmean = lax.psum(jnp.sum(cap_var, axis=1), 'hour') / hours_all  102 us
    reduce_scatter x8, waiting for transfers between devices, shards(): lax.psum_scatter(partial_rows, 'reg', scatter_dimension=2, tiled=True)  64.9 us
    all_gather x7, blocking collectives, shards(): lax.all_gather(dual_var.astype(jnp.bfloat16), 'reg', axis=2, tiled=True)  46.4 us
    dot_general x8, matrix products, shards(): jnp.einsum('shr,rc->shc', dual_low, matrix, preferred_element_type=jnp.fl...  32.9 us
    ppermute x8, starting transfers between devices, with_halo(): lax.ppermute(tail, axis, [(i, (i + 1) % count) for i in range(ends)])  27.1 us
    dot_general x8, matrix products, shards(): jnp.einsum('shc,rc->shr', primal_ext.astype(jnp.bfloat16), matrix, prefer...  11.9 us
    ppermute x8, starting transfers between devices, with_halo(): lax.ppermute(head, axis, [((i + 1) % count, i) for i in range(ends)])  10.3 us
    psum x1, blocking collectives, shards(): sum_total, mass_total = lax.psum((node_sum, node_mass), 'scen')  8.32 us
  transfers between devices with their start and end apart: 24, of which 8 were waited for; matrix products, arithmetic and copies ran while one was open for 5% of the time, Pallas kernels for 0%

commit v1 on v0

--- a/solution.py
+++ b/solution.py
@@ -10,6 +10,11 @@
 STEP_INVEST = 0.5
 STEP_DUAL = 0.3
 STEP_CAP = 0.05
+
+
+def gather_and_add(x, mesh_axis):
+    parts = lax.all_gather(x, mesh_axis)
+    return jnp.sum(parts, axis=0)
 
 
 def with_halo(cells, sides, width):
@@ -66,7 +71,7 @@
         rough = 2.0 * primal - padded[:, :-2] - padded[:, 2:]
         pulled = jnp.einsum("shr,rc->shc", dual_low, matrix, preferred_element_type=jnp.float32)
         grad_x = cost_rate + RAMP_WEIGHT * rough - pulled + cap_var
-        zmean = lax.psum(jnp.sum(cap_var, axis=1), "hour") / hours_all
+        zmean = gather_and_add(jnp.sum(cap_var, axis=1), "hour") / hours_all
         grad_u = invest_cost[None] + multiplier + PENALTY * (invest - consensus) - zmean[:, None, :]
         primal_new = jnp.maximum(primal - STEP_PRIMAL * grad_x, 0.0)
         invest_new = jnp.maximum(invest - STEP_INVEST * grad_u, 0.0)

time: 346 us -> 350 us (1.012)
  blocking collectives: 157 us -> 161 us
    all_gather x0 -> x8, blocking collectives: none -> 107 us  [gather_and_add(): parts = lax.all_gather(x, mesh_axis)]
    psum x8 -> x0, blocking collectives: 102 us -> none  [shards(): zmean = lax.psum(jnp.sum(cap_var, axis=1), 'hour') / hours_all]
where the time goes in v1:
time: 350 us; the launch traced here: 348 us
  blocking collectives  161 us (46%)
  waiting for transfers between devices  62.5 us (18%)
  matrix products  46.1 us (13%)
  starting transfers between devices  40.1 us (11%)
  between operations  14.7 us (4%)
  local copies, waits for them, and re-layouts  11.8 us (3%)
  other arithmetic  11.6 us (3%)
    all_gather x8, blocking collectives, gather_and_add(): parts = lax.all_gather(x, mesh_axis)  107 us
    reduce_scatter x8, waiting for transfers between devices, shards(): lax.psum_scatter(partial_rows, 'reg', scatter_dimension=2, tiled=True)  62.4 us
    all_gather x7, blocking collectives, shards(): lax.all_gather(dual_var.astype(jnp.bfloat16), 'reg', axis=2, tiled=True)  46.4 us
    dot_general x8, matrix products, shards(): jnp.einsum('shr,rc->shc', dual_low, matrix, preferred_element_type=jnp.fl...  32.9 us
    ppermute x8, starting transfers between devices, with_halo(): lax.ppermute(tail, axis, [(i, (i + 1) % count) for i in range(ends)])  29.4 us
    dot_general x8, matrix products, shards(): jnp.einsum('shc,rc->shr', primal_ext.astype(jnp.bfloat16), matrix, prefer...  11.9 us
    ppermute x8, starting transfers between devices, with_halo(): lax.ppermute(head, axis, [((i + 1) % count, i) for i in range(ends)])  10.3 us
    psum x1, blocking collectives, shards(): sum_total, mass_total = lax.psum((node_sum, node_mass), 'scen')  8.3 us
  transfers between devices with their start and end apart: 24, of which 8 were waited for; matrix products, arithmetic and copies ran while one was open for 5% of the time, Pallas kernels for 0%

profile of v1, /device:TPU:0, one launch (start us, length us, event | category | flops | bytes accessed | tf_op | source)
XLA Modules:
  0.0 348.3 jit_solution(10665701522728707048)
XLA Ops:
  8.3 5.0 %collective-permute-start = (f32[4,1,512]{2,1,0:T(1,128)S(1)}, f32[4,1,512]{2,1,0:T(1,128)S(1)}, u32[]{:S(2)}, u32[]{:S(2)}) collective-permute-start(f32[4,1,512]{2,1,0:T(1,128)S(1)} %get-tuple-element.40), channel_id=1, source_target_pairs={{0,4},{4,8},{8,12},{1,5},{5,9},{9,13},{2,6},{6,10},{10,14},{3,7},{... | collective-permute-start | bytes 24584 | tf_op jit(solution)/shard_map/ppermute | solution.py:28
  13.3 1.3 collective-permute-start.1
  14.6 1.5 reduce_sum.207
  16.1 14.4 %all-gather.8 = f32[4,4,512]{2,1,0:T(4,128)S(1)} all-gather(f32[1,4,512]{2,1,0:T(4,128)S(1)} %bitcast.93), channel_id=2, replica_groups=mesh['scen'=2,'hour'=4,'reg'=4] {'hour'}, dimensions={0}, use_global_device_ids=true | all-gather | bytes 40960 | tf_op jit(solution)/shard_map/all_gather | solution.py:16
  30.7 5.6 %fusion.161 = (f32[4,512]{1,0:T(4,128)S(1)}, f32[4,168,512]{2,1,0:T(8,128)}, f32[4,168,512]{2,1,0:T(8,128)S(1)}) fusion(f32[4,168,512]{2,1,0:T(8,128)} %param.20, f32[4,512]{1,0:T(4,128)S(1)} %get-tuple-element.24, f32[4,168,512]{2,1,0:T(8,128)} %param.18, f32[4,168,256]{2,1,0:T(8,128)S(1)} %copy-done.19, ...), kind=kOutput, calls=%fused_computation.216 | convolution fusion | flops 182867968 | bytes 7864320 | tf_op jit(solution)/shard_map/shr,rc->shc/dot_general | solution.py:72
  36.3 1.5 fusion.87
  38.3 1.1 constant_dynamic-slice_fusion.1
  39.6 13.1 %all-gather.9 = f32[4,4,512]{2,1,0:T(4,128)S(1)} all-gather(f32[1,4,512]{2,1,0:T(4,128)S(1)} %bitcast.95), channel_id=3, replica_groups=mesh['scen'=2,'hour'=4,'reg'=4] {'hour'}, dimensions={0}, use_global_device_ids=true | all-gather | bytes 40960 | tf_op jit(solution)/shard_map/all_gather | solution.py:16
  52.8 3.5 %collective-permute-start.2 = (f32[4,1,512]{2,1,0:T(1,128)S(1)}, f32[4,1,512]{2,1,0:T(1,128)S(1)}, u32[]{:S(2)}, u32[]{:S(2)}) collective-permute-start(f32[4,1,512]{2,1,0:T(1,128)S(1)} %get-tuple-element.38), channel_id=1, source_target_pairs={{0,4},{4,8},{8,12},{1,5},{5,9},{9,13},{2,6},{6,10},{10,14},{3,7},{... | collective-permute-start | bytes 24584 | tf_op jit(solution)/shard_map/ppermute | solution.py:28
  56.3 1.3 collective-permute-start.3
  57.6 6.2 %reduce-scatter.9.cloned.1.call-done = f32[4,168,64]{1,2,0:T(8,128)} async-done(((f32[4,168,256]{1,2,0:T(8,128)}), f32[4,168,64]{1,2,0:T(8,128)}) %reduce-scatter.9.cloned.1.call-update) | async-done | bytes 172048 | tf_op jit(solution)/shard_map/reduce_scatter | solution.py:86
  63.8 1.1 fusion.131
  65.0 6.6 %all_gather.69 = bf16[4,168,256]{1,2,0:T(8,128)(2,1)S(1)} all-gather(bf16[4,168,64]{1,2,0:T(8,128)(2,1)S(1)} %fusion.131), channel_id=1, replica_groups=mesh['scen'=2,'hour'=4,'reg'=4] {'reg'}, dimensions={2}, use_global_device_ids=true | all-gather | bytes 430080 | tf_op jit(solution)/shard_map/all_gather | solution.py:89
  71.6 3.6 %fusion.159 = (f32[4,512]{1,0:T(4,128)S(1)}, f32[4,168,512]{2,1,0:T(8,128)}, f32[4,168,512]{2,1,0:T(8,128)S(1)}) fusion(f32[4,168,512]{2,1,0:T(8,128)} %get-tuple-element.23, f32[4,512]{1,0:T(4,128)S(1)} %subtract_reduce_fusion.5, f32[4,168,512]{2,1,0:T(8,128)S(1)} %get-tuple-element.42, bf16[4,168,256]{1,2,0:T(8,128)(2,1)S(1)} %all_gather.69, ...), kind=kOutput, calls=%fused_computation.214 | convolution fusion | flops 182695936 | bytes 7520256 | tf_op jit(solution)/shard_map/shr,rc->shc/dot_general | solution.py:72
  75.2 1.1 copy-done.1
  76.2 1.5 fusion.85
  77.8 13.3 %all-gather.10 = f32[4,4,512]{2,1,0:T(4,128)S(1)} all-gather(f32[1,4,512]{2,1,0:T(4,128)S(1)} %bitcast.96), channel_id=4, replica_groups=mesh['scen'=2,'hour'=4,'reg'=4] {'hour'}, dimensions={0}, use_global_device_ids=true | all-gather | bytes 40960 | tf_op jit(solution)/shard_map/all_gather | solution.py:16
  92.0 3.4 collective-permute-start.4
  95.5 1.3 collective-permute-start.5
  96.8 6.4 %reduce-scatter.11.cloned.1.call-done = f32[4,168,64]{1,2,0:T(8,128)} async-done(((f32[4,168,256]{1,2,0:T(8,128)}), f32[4,168,64]{1,2,0:T(8,128)}) %reduce-scatter.11.cloned.1.call-update) | async-done | bytes 172048 | tf_op jit(solution)/shard_map/reduce_scatter | solution.py:86
  104.3 6.6 %all_gather.72 = bf16[4,168,256]{1,2,0:T(8,128)(2,1)S(1)} all-gather(bf16[4,168,64]{1,2,0:T(8,128)(2,1)S(1)} %get-tuple-element.20), channel_id=1, replica_groups=mesh['scen'=2,'hour'=4,'reg'=4] {'reg'}, dimensions={2}, use_global_device_ids=true | all-gather | bytes 430080 | tf_op jit(solution)/shard_map/all_gather | solution.py:89
  110.9 4.0 %fusion.158 = (f32[4,512]{1,0:T(4,128)S(1)}, f32[4,168,512]{2,1,0:T(8,128)}, f32[4,168,512]{2,1,0:T(8,128)S(1)}) fusion(f32[4,168,512]{2,1,0:T(8,128)} %get-tuple-element.19, f32[4,512]{1,0:T(4,128)S(1)} %subtract_reduce_fusion.4, f32[4,168,512]{2,1,0:T(8,128)S(1)} %copy-done.2, bf16[4,168,256]{1,2,0:T(8,128)(2,1)S(1)} %all_gather.72, ...), kind=kOutput, calls=%fused_computation.213 | convolution fusion | flops 182695936 | bytes 7520256 | tf_op jit(solution)/shard_map/shr,rc->shc/dot_general | solution.py:72
  116.0 1.5 fusion.83
  117.6 13.2 %all-gather.11 = f32[4,4,512]{2,1,0:T(4,128)S(1)} all-gather(f32[1,4,512]{2,1,0:T(4,128)S(1)} %bitcast.97), channel_id=5, replica_groups=mesh['scen'=2,'hour'=4,'reg'=4] {'hour'}, dimensions={0}, use_global_device_ids=true | all-gather | bytes 40960 | tf_op jit(solution)/shard_map/all_gather | solution.py:16
  131.7 3.4 collective-permute-start.6
  135.1 1.3 collective-permute-start.7
  136.4 6.6 %reduce-scatter.13.cloned.1.call-done = f32[4,168,64]{1,2,0:T(8,128)} async-done(((f32[4,168,256]{1,2,0:T(8,128)}), f32[4,168,64]{1,2,0:T(8,128)}) %reduce-scatter.13.cloned.1.call-update) | async-done | bytes 172048 | tf_op jit(solution)/shard_map/reduce_scatter | solution.py:86
  144.0 6.6 %all_gather.75 = bf16[4,168,256]{1,2,0:T(8,128)(2,1)S(1)} all-gather(bf16[4,168,64]{1,2,0:T(8,128)(2,1)S(1)} %fusion.132), channel_id=1, replica_groups=mesh['scen'=2,'hour'=4,'reg'=4] {'reg'}, dimensions={2}, use_global_device_ids=true | all-gather | bytes 430080 | tf_op jit(solution)/shard_map/all_gather | solution.py:89
  150.6 5.4 %fusion.156 = (f32[4,512]{1,0:T(4,128)S(1)}, f32[4,168,512]{2,1,0:T(8,128)}, f32[4,168,512]{2,1,0:T(8,128)S(1)}) fusion(f32[4,168,512]{2,1,0:T(8,128)} %get-tuple-element.17, f32[4,512]{1,0:T(4,128)S(1)} %subtract_reduce_fusion.3, f32[4,168,512]{2,1,0:T(8,128)} %copy-done.3, bf16[4,168,256]{1,2,0:T(8,128)(2,1)S(1)} %all_gather.75, ...), kind=kOutput, calls=%fused_computation.211 | convolution fusion | flops 182695936 | bytes 7520256 | tf_op jit(solution)/shard_map/shr,rc->shc/dot_general | solution.py:72
  156.0 1.5 fusion.81
  157.6 13.2 %all-gather.12 = f32[4,4,512]{2,1,0:T(4,128)S(1)} all-gather(f32[1,4,512]{2,1,0:T(4,128)S(1)} %bitcast.98), channel_id=6, replica_groups=mesh['scen'=2,'hour'=4,'reg'=4] {'hour'}, dimensions={0}, use_global_device_ids=true | all-gather | bytes 40960 | tf_op jit(solution)/shard_map/all_gather | solution.py:16
  170.8 3.4 collective-permute-start.8
  174.2 1.3 collective-permute-start.9
  175.6 7.4 %reduce-scatter.15.cloned.1.call-done = f32[4,168,64]{1,2,0:T(8,128)} async-done(((f32[4,168,256]{1,2,0:T(8,128)}), f32[4,168,64]{1,2,0:T(8,128)}) %reduce-scatter.15.cloned.1.call-update) | async-done | bytes 172048 | tf_op jit(solution)/shard_map/reduce_scatter | solution.py:86
  183.0 1.1 fusion.157
  184.1 6.8 %all_gather.78 = bf16[4,168,256]{1,2,0:T(8,128)(2,1)S(1)} all-gather(bf16[4,168,64]{1,2,0:T(8,128)(2,1)S(1)} %get-tuple-element.14), channel_id=1, replica_groups=mesh['scen'=2,'hour'=4,'reg'=4] {'reg'}, dimensions={2}, use_global_device_ids=true | all-gather | bytes 430080 | tf_op jit(solution)/shard_map/all_gather | solution.py:89
  190.9 3.6 %fusion.155 = (f32[4,512]{1,0:T(4,128)S(1)}, f32[4,168,512]{2,1,0:T(8,128)}, f32[4,168,512]{2,1,0:T(8,128)S(1)}) fusion(f32[4,168,512]{2,1,0:T(8,128)} %get-tuple-element.13, f32[4,512]{1,0:T(4,128)S(1)} %subtract_reduce_fusion.2, f32[4,168,512]{2,1,0:T(8,128)S(1)} %get-tuple-element.45, bf16[4,168,256]{1,2,0:T(8,128)(2,1)S(1)} %all_gather.78, ...), kind=kOutput, calls=%fused_computation.210 | convolution fusion | flops 182695936 | bytes 7520256 | tf_op jit(solution)/shard_map/shr,rc->shc/dot_general | solution.py:72
  195.6 1.5 fusion.79
  197.2 13.2 %all-gather.13 = f32[4,4,512]{2,1,0:T(4,128)S(1)} all-gather(f32[1,4,512]{2,1,0:T(4,128)S(1)} %bitcast.99), channel_id=7, replica_groups=mesh['scen'=2,'hour'=4,'reg'=4] {'hour'}, dimensions={0}, use_global_device_ids=true | all-gather | bytes 40960 | tf_op jit(solution)/shard_map/all_gather | solution.py:16
  211.2 3.4 collective-permute-start.10
  214.7 1.3 collective-permute-start.11
  216.1 6.5 %reduce-scatter.17.cloned.1.call-done = f32[4,168,64]{1,2,0:T(8,128)} async-done(((f32[4,168,256]{1,2,0:T(8,128)}), f32[4,168,64]{1,2,0:T(8,128)}) %reduce-scatter.17.cloned.1.call-update) | async-done | bytes 172048 | tf_op jit(solution)/shard_map/reduce_scatter | solution.py:86
  223.6 6.6 %all_gather.81 = bf16[4,168,256]{1,2,0:T(8,128)(2,1)S(1)} all-gather(bf16[4,168,64]{1,2,0:T(8,128)(2,1)S(1)} %fusion.133), channel_id=1, replica_groups=mesh['scen'=2,'hour'=4,'reg'=4] {'reg'}, dimensions={2}, use_global_device_ids=true | all-gather | bytes 430080 | tf_op jit(solution)/shard_map/all_gather | solution.py:89
  230.2 5.4 %fusion.153 = (f32[4,512]{1,0:T(4,128)S(1)}, f32[4,168,512]{2,1,0:T(8,128)}, f32[4,168,512]{2,1,0:T(8,128)S(1)}) fusion(f32[4,168,512]{2,1,0:T(8,128)} %get-tuple-element.11, f32[4,512]{1,0:T(4,128)S(1)} %subtract_reduce_fusion.1, f32[4,168,512]{2,1,0:T(8,128)} %copy-done.5, bf16[4,168,256]{1,2,0:T(8,128)(2,1)S(1)} %all_gather.81, ...), kind=kOutput, calls=%fused_computation.208 | convolution fusion | flops 182695936 | bytes 7520256 | tf_op jit(solution)/shard_map/shr,rc->shc/dot_general | solution.py:72
  235.6 1.5 fusion.77
  237.2 13.2 %all-gather.14 = f32[4,4,512]{2,1,0:T(4,128)S(1)} all-gather(f32[1,4,512]{2,1,0:T(4,128)S(1)} %bitcast.100), channel_id=8, replica_groups=mesh['scen'=2,'hour'=4,'reg'=4] {'hour'}, dimensions={0}, use_global_device_ids=true | all-gather | bytes 40960 | tf_op jit(solution)/shard_map/all_gather | solution.py:16
  250.4 4.0 %collective-permute-start.12 = (f32[4,1,512]{2,1,0:T(1,128)S(1)}, f32[4,1,512]{2,1,0:T(1,128)}, u32[]{:S(2)}, u32[]{:S(2)}) collective-permute-start(f32[4,1,512]{2,1,0:T(1,128)S(1)} %get-tuple-element.28), channel_id=1, source_target_pairs={{0,4},{4,8},{8,12},{1,5},{5,9},{9,13},{2,6},{6,10},{10,14},{3,7},{... | collective-permute-start | bytes 24584 | tf_op jit(solution)/shard_map/ppermute | solution.py:28
  254.4 1.3 collective-permute-start.13
  255.8 6.8 %reduce-scatter.19.cloned.1.call-done = f32[4,168,64]{1,2,0:T(8,128)} async-done(((f32[4,168,256]{1,2,0:T(8,128)}), f32[4,168,64]{1,2,0:T(8,128)}) %reduce-scatter.19.cloned.1.call-update) | async-done | bytes 172048 | tf_op jit(solution)/shard_map/reduce_scatter | solution.py:86
  262.6 1.1 fusion.154
  263.7 6.6 %all_gather.84 = bf16[4,168,256]{1,2,0:T(8,128)(2,1)S(1)} all-gather(bf16[4,168,64]{1,2,0:T(8,128)(2,1)S(1)} %get-tuple-element.8), channel_id=1, replica_groups=mesh['scen'=2,'hour'=4,'reg'=4] {'reg'}, dimensions={2}, use_global_device_ids=true | all-gather | bytes 430080 | tf_op jit(solution)/shard_map/all_gather | solution.py:89
  270.4 2.5 fusion.130
  274.0 1.5 fusion.75
  276.4 3.4 collective-permute-start.14
  279.8 1.3 collective-permute-start.15
  281.1 19.9 %reduce-scatter.21.cloned.1.call-done = f32[4,168,64]{1,2,0:T(8,128)} async-done(((f32[4,168,256]{1,2,0:T(8,128)}), f32[4,168,64]{1,2,0:T(8,128)}) %reduce-scatter.21.cloned.1.call-update) | async-done | bytes 172048 | tf_op jit(solution)/shard_map/reduce_scatter | solution.py:86
  301.0 1.1 fusion.134
  302.1 6.6 %all_gather.87 = bf16[4,168,256]{1,2,0:T(8,128)(2,1)S(1)} all-gather(bf16[4,168,64]{1,2,0:T(8,128)(2,1)S(1)} %fusion.134), channel_id=1, replica_groups=mesh['scen'=2,'hour'=4,'reg'=4] {'reg'}, dimensions={2}, use_global_device_ids=true | all-gather | bytes 430080 | tf_op jit(solution)/shard_map/all_gather | solution.py:89
  308.7 2.8 fusion.7
  312.7 1.5 fusion.74
  314.4 13.2 %all-gather.15 = f32[4,4,512]{2,1,0:T(4,128)S(1)} all-gather(f32[1,4,512]{2,1,0:T(4,128)S(1)} %bitcast.94), channel_id=9, replica_groups=mesh['scen'=2,'hour'=4,'reg'=4] {'hour'}, dimensions={0}, use_global_device_ids=true | all-gather | bytes 40960 | tf_op jit(solution)/shard_map/all_gather | solution.py:16
  328.0 8.3 %all-reduce = (f32[3,4,512]{2,1,0:T(4,128)S(1)}, f32[3,4]{1,0:T(4,128)S(1)}) all-reduce(f32[3,4,512]{2,1,0:T(4,128)S(1)} %fusion.135, f32[3,4]{1,0:T(4,128)S(1)} %bitcast.101), channel_id=1, replica_groups=mesh['scen'=2,'hour'=4,'reg'=4] {'scen'}, use_global_device_ids=true, to_apply=%region_31.0 | all-reduce | flops 6156 | bytes 49248 | tf_op jit(solution)/shard_map/psum | solution.py:101
  337.1 2.6 reduce-scatter.23.cloned.1.call-done
  339.7 1.7 add_maximum_fusion.7
  (131 shorter events, 15.3 us)
Async XLA Ops:
  7.2 30.7 %copy-start = (f32[4,168,256]{2,1,0:T(8,128)S(1)}, f32[4,168,256]{2,1,0:T(8,128)}, u32[]{:S(2)}) copy-start(f32[4,168,256]{2,1,0:T(8,128)} %param.17) | copy-start | bytes 2064388
  7.2 23.3 %copy-start.18 = (bf16[1,256,512]{2,1,0:T(8,128)(2,1)S(1)}, bf16[1,256,512]{2,1,0:T(8,128)(2,1)}, u32[]{:S(2)}) copy-start(bf16[1,256,512]{2,1,0:T(8,128)(2,1)} %param.15) | copy-start | bytes 786436
  7.2 23.3 %copy-start.17 = (s32[1,256,512]{2,1,0:T(8,128)S(1)}, s32[1,256,512]{2,1,0:T(8,128)}, u32[]{:S(2)}) copy-start(s32[1,256,512]{2,1,0:T(8,128)} %param.16) | copy-start | bytes 1572868
  7.2 23.4 %copy-start.22 = (f32[3,512]{1,0:T(4,128)S(1)}, f32[3,512]{1,0:T(4,128)}, u32[]{:S(2)}) copy-start(f32[3,512]{1,0:T(4,128)} %param.14) | copy-start | bytes 18436
  7.2 23.4 %copy-start.9 = (f32[4,3,512]{2,0,1:T(4,128)S(1)}, f32[4,3,512]{2,0,1:T(4,128)}, u32[]{:S(2)}) copy-start(f32[4,3,512]{2,0,1:T(4,128)} %param.21) | copy-start | bytes 73732
  7.2 23.4 %copy-start.21 = (f32[4,3,512]{2,0,1:T(4,128)S(1)}, f32[4,3,512]{2,0,1:T(4,128)}, u32[]{:S(2)}) copy-start(f32[4,3,512]{2,0,1:T(4,128)} %param.22) | copy-start | bytes 73732
  7.2 23.4 %copy-start.10 = (f32[4,3,512]{2,0,1:T(4,128)S(1)}, f32[4,3,512]{2,0,1:T(4,128)}, u32[]{:S(2)}) copy-start(f32[4,3,512]{2,0,1:T(4,128)} %param.23) | copy-start | bytes 73732
  7.2 23.4 %copy-start.19 = (f32[4,168,256]{2,1,0:T(8,128)S(1)}, f32[4,168,256]{2,1,0:T(8,128)}, u32[]{:S(2)}) copy-start(f32[4,168,256]{2,1,0:T(8,128)} %param.19) | copy-start | bytes 2064388
  7.3 56.6 %reduce-scatter.9.cloned.1.call-start = ((), (), s32[]{:S(2)}) async-start(), calls=%async_computation.8 | async-start | bytes 1310720 | tf_op jit(solution)/shard_map/reduce_scatter | solution.py:86
  8.3 22.4 %collective-permute-start = (f32[4,1,512]{2,1,0:T(1,128)S(1)}, f32[4,1,512]{2,1,0:T(1,128)S(1)}, u32[]{:S(2)}, u32[]{:S(2)}) collective-permute-start(f32[4,1,512]{2,1,0:T(1,128)S(1)} %get-tuple-element.40), channel_id=1, source_target_pairs={{0,4},{4,8},{8,12},{1,5},{5,9},{9,13},{2,6},{6,10},{10,14},{3,7},{... | collective-permute-start | bytes 24584 | tf_op jit(solution)/shard_map/ppermute | solution.py:28
  13.3 17.4 %collective-permute-start.1 = (f32[4,1,512]{2,1,0:T(1,128)S(1)}, f32[4,1,512]{2,1,0:T(1,128)S(1)}, u32[]{:S(2)}, u32[]{:S(2)}) collective-permute-start(f32[4,1,512]{2,1,0:T(1,128)S(1)} %get-tuple-element.41), channel_id=1, source_target_pairs={{4,0},{8,4},{12,8},{5,1},{9,5},{13,9},{6,2},{10,6},{14,10},{7,3},{... | collective-permute-start | bytes 24584 | tf_op jit(solution)/shard_map/ppermute | solution.py:30
  30.7 5.6 %copy-start.11 = (f32[4,168,512]{2,1,0:T(8,128)S(1)}, f32[4,168,512]{2,1,0:T(8,128)}, u32[]{:S(2)}) copy-start(f32[4,168,512]{2,1,0:T(8,128)} %param.18) | copy-start | bytes 4128772
  37.9 65.4 %reduce-scatter.11.cloned.1.call-start = ((), (), s32[]{:S(2)}) async-start(), calls=%async_computation.9 | async-start | bytes 1310720 | tf_op jit(solution)/shard_map/reduce_scatter | solution.py:86
  52.8 18.8 %collective-permute-start.2 = (f32[4,1,512]{2,1,0:T(1,128)S(1)}, f32[4,1,512]{2,1,0:T(1,128)S(1)}, u32[]{:S(2)}, u32[]{:S(2)}) collective-permute-start(f32[4,1,512]{2,1,0:T(1,128)S(1)} %get-tuple-element.38), channel_id=1, source_target_pairs={{0,4},{4,8},{8,12},{1,5},{5,9},{9,13},{2,6},{6,10},{10,14},{3,7},{... | collective-permute-start | bytes 24584 | tf_op jit(solution)/shard_map/ppermute | solution.py:28
  56.3 15.3 %collective-permute-start.3 = (f32[4,1,512]{2,1,0:T(1,128)S(1)}, f32[4,1,512]{2,1,0:T(1,128)S(1)}, u32[]{:S(2)}, u32[]{:S(2)}) collective-permute-start(f32[4,1,512]{2,1,0:T(1,128)S(1)} %get-tuple-element.39), channel_id=1, source_target_pairs={{4,0},{8,4},{12,8},{5,1},{9,5},{13,9},{6,2},{10,6},{14,10},{7,3},{... | collective-permute-start | bytes 24584 | tf_op jit(solution)/shard_map/ppermute | solution.py:30
  63.8 7.7 %copy-start.23 = (f32[4,168,512]{2,1,0:T(8,128)S(1)}, f32[4,168,512]{2,1,0:T(8,128)}, u32[]{:S(2)}) copy-start(f32[4,168,512]{2,1,0:T(8,128)} %param.13) | copy-start | bytes 4128772
  75.2 1.1 copy-start.1
  77.7 25.5 %copy-start.14 = (f32[4,168,64]{1,2,0:T(8,128)S(1)}, f32[4,168,64]{1,2,0:T(8,128)}, u32[]{:S(2)}) copy-start(f32[4,168,64]{1,2,0:T(8,128)} %reduce-scatter.9.cloned.1.call-done) | copy-start | bytes 516100
  77.8 33.2 %copy-start.2 = (f32[4,168,512]{2,1,0:T(8,128)S(1)}, f32[4,168,512]{2,1,0:T(8,128)}, u32[]{:S(2)}) copy-start(f32[4,168,512]{2,1,0:T(8,128)} %copy-done.1) | copy-start | bytes 4128772
  77.8 65.2 %reduce-scatter.13.cloned.1.call-start = ((), (), s32[]{:S(2)}) async-start(), calls=%async_computation.10 | async-start | bytes 1310720 | tf_op jit(solution)/shard_map/reduce_scatter | solution.py:86
  92.0 18.9 %collective-permute-start.4 = (f32[4,1,512]{2,1,0:T(1,128)S(1)}, f32[4,1,512]{2,1,0:T(1,128)S(1)}, u32[]{:S(2)}, u32[]{:S(2)}) collective-permute-start(f32[4,1,512]{2,1,0:T(1,128)S(1)} %get-tuple-element.36), channel_id=1, source_target_pairs={{0,4},{4,8},{8,12},{1,5},{5,9},{9,13},{2,6},{6,10},{10,14},{3,7},{... | collective-permute-start | bytes 24584 | tf_op jit(solution)/shard_map/ppermute | solution.py:28
  95.5 15.5 %collective-permute-start.5 = (f32[4,1,512]{2,1,0:T(1,128)S(1)}, f32[4,1,512]{2,1,0:T(1,128)S(1)}, u32[]{:S(2)}, u32[]{:S(2)}) collective-permute-start(f32[4,1,512]{2,1,0:T(1,128)S(1)} %get-tuple-element.37), channel_id=1, source_target_pairs={{4,0},{8,4},{12,8},{5,1},{9,5},{13,9},{6,2},{10,6},{14,10},{7,3},{... | collective-permute-start | bytes 24584 | tf_op jit(solution)/shard_map/ppermute | solution.py:30
  114.9 1.1 copy-start.3
  117.5 65.5 %reduce-scatter.15.cloned.1.call-start = ((), (), s32[]{:S(2)}) async-start(), calls=%async_computation.11 | async-start | bytes 1310720 | tf_op jit(solution)/shard_map/reduce_scatter | solution.py:86
  131.7 19.0 %collective-permute-start.6 = (f32[4,1,512]{2,1,0:T(1,128)S(1)}, f32[4,1,512]{2,1,0:T(1,128)S(1)}, u32[]{:S(2)}, u32[]{:S(2)}) collective-permute-start(f32[4,1,512]{2,1,0:T(1,128)S(1)} %get-tuple-element.34), channel_id=1, source_target_pairs={{0,4},{4,8},{8,12},{1,5},{5,9},{9,13},{2,6},{6,10},{10,14},{3,7},{... | collective-permute-start | bytes 24584 | tf_op jit(solution)/shard_map/ppermute | solution.py:28
  135.1 15.6 %collective-permute-start.7 = (f32[4,1,512]{2,1,0:T(1,128)S(1)}, f32[4,1,512]{2,1,0:T(1,128)S(1)}, u32[]{:S(2)}, u32[]{:S(2)}) collective-permute-start(f32[4,1,512]{2,1,0:T(1,128)S(1)} %get-tuple-element.35), channel_id=1, source_target_pairs={{4,0},{8,4},{12,8},{5,1},{9,5},{13,9},{6,2},{10,6},{14,10},{7,3},{... | collective-permute-start | bytes 24584 | tf_op jit(solution)/shard_map/ppermute | solution.py:30
  150.6 5.4 %copy-start.4 = (f32[4,168,512]{2,1,0:T(8,128)S(1)}, f32[4,168,512]{2,1,0:T(8,128)}, u32[]{:S(2)}) copy-start(f32[4,168,512]{2,1,0:T(8,128)} %copy-done.3) | copy-start | bytes 4128772
  157.5 25.5 %copy-start.15 = (f32[4,168,64]{1,2,0:T(8,128)S(1)}, f32[4,168,64]{1,2,0:T(8,128)}, u32[]{:S(2)}) copy-start(f32[4,168,64]{1,2,0:T(8,128)} %reduce-scatter.13.cloned.1.call-done) | copy-start | bytes 516100
  157.5 65.1 %reduce-scatter.17.cloned.1.call-start = ((), (), s32[]{:S(2)}) async-start(), calls=%async_computation.12 | async-start | bytes 1310720 | tf_op jit(solution)/shard_map/reduce_scatter | solution.py:86
  170.8 20.1 %collective-permute-start.8 = (f32[4,1,512]{2,1,0:T(1,128)S(1)}, f32[4,1,512]{2,1,0:T(1,128)S(1)}, u32[]{:S(2)}, u32[]{:S(2)}) collective-permute-start(f32[4,1,512]{2,1,0:T(1,128)S(1)} %get-tuple-element.32), channel_id=1, source_target_pairs={{0,4},{4,8},{8,12},{1,5},{5,9},{9,13},{2,6},{6,10},{10,14},{3,7},{... | collective-permute-start | bytes 24584 | tf_op jit(solution)/shard_map/ppermute | solution.py:28
  174.2 16.7 %collective-permute-start.9 = (f32[4,1,512]{2,1,0:T(1,128)S(1)}, f32[4,1,512]{2,1,0:T(1,128)S(1)}, u32[]{:S(2)}, u32[]{:S(2)}) collective-permute-start(f32[4,1,512]{2,1,0:T(1,128)S(1)} %get-tuple-element.33), channel_id=1, source_target_pairs={{4,0},{8,4},{12,8},{5,1},{9,5},{13,9},{6,2},{10,6},{14,10},{7,3},{... | collective-permute-start | bytes 24584 | tf_op jit(solution)/shard_map/ppermute | solution.py:30
  183.0 7.9 %copy-start.24 = (f32[4,168,512]{2,1,0:T(8,128)S(1)}, f32[4,168,512]{2,1,0:T(8,128)}, u32[]{:S(2)}) copy-start(f32[4,168,512]{2,1,0:T(8,128)} %param.13) | copy-start | bytes 4128772
  194.5 1.1 copy-start.5
  197.1 65.5 %reduce-scatter.19.cloned.1.call-start = ((), (), s32[]{:S(2)}) async-start(), calls=%async_computation.13 | async-start | bytes 1310720 | tf_op jit(solution)/shard_map/reduce_scatter | solution.py:86
  211.2 19.0 %collective-permute-start.10 = (f32[4,1,512]{2,1,0:T(1,128)S(1)}, f32[4,1,512]{2,1,0:T(1,128)S(1)}, u32[]{:S(2)}, u32[]{:S(2)}) collective-permute-start(f32[4,1,512]{2,1,0:T(1,128)S(1)} %get-tuple-element.30), channel_id=1, source_target_pairs={{0,4},{4,8},{8,12},{1,5},{5,9},{9,13},{2,6},{6,10},{10,14},{3,7},{... | collective-permute-start | bytes 24584 | tf_op jit(solution)/shard_map/ppermute | solution.py:28
  214.7 15.6 %collective-permute-start.11 = (f32[4,1,512]{2,1,0:T(1,128)S(1)}, f32[4,1,512]{2,1,0:T(1,128)S(1)}, u32[]{:S(2)}, u32[]{:S(2)}) collective-permute-start(f32[4,1,512]{2,1,0:T(1,128)S(1)} %get-tuple-element.31), channel_id=1, source_target_pairs={{4,0},{8,4},{12,8},{5,1},{9,5},{13,9},{6,2},{10,6},{14,10},{7,3},{... | collective-permute-start | bytes 24584 | tf_op jit(solution)/shard_map/ppermute | solution.py:30
  230.2 5.4 %copy-start.6 = (f32[4,168,512]{2,1,0:T(8,128)S(1)}, f32[4,168,512]{2,1,0:T(8,128)}, u32[]{:S(2)}) copy-start(f32[4,168,512]{2,1,0:T(8,128)} %copy-done.5) | copy-start | bytes 4128772
  237.1 25.5 %copy-start.16 = (f32[4,168,64]{1,2,0:T(8,128)S(1)}, f32[4,168,64]{1,2,0:T(8,128)}, u32[]{:S(2)}) copy-start(f32[4,168,64]{1,2,0:T(8,128)} %reduce-scatter.17.cloned.1.call-done) | copy-start | bytes 516100
  237.1 63.9 %reduce-scatter.21.cloned.1.call-start = ((), (), s32[]{:S(2)}) async-start(), calls=%async_computation.14 | async-start | bytes 1310720 | tf_op jit(solution)/shard_map/reduce_scatter | solution.py:86
  250.4 20.0 %collective-permute-start.12 = (f32[4,1,512]{2,1,0:T(1,128)S(1)}, f32[4,1,512]{2,1,0:T(1,128)}, u32[]{:S(2)}, u32[]{:S(2)}) collective-permute-start(f32[4,1,512]{2,1,0:T(1,128)S(1)} %get-tuple-element.28), channel_id=1, source_target_pairs={{0,4},{4,8},{8,12},{1,5},{5,9},{9,13},{2,6},{6,10},{10,14},{3,7},{... | collective-permute-start | bytes 24584 | tf_op jit(solution)/shard_map/ppermute | solution.py:28
  254.4 16.0 %collective-permute-start.13 = (f32[4,1,512]{2,1,0:T(1,128)S(1)}, f32[4,1,512]{2,1,0:T(1,128)}, u32[]{:S(2)}, u32[]{:S(2)}) collective-permute-start(f32[4,1,512]{2,1,0:T(1,128)S(1)} %get-tuple-element.29), channel_id=1, source_target_pairs={{4,0},{8,4},{12,8},{5,1},{9,5},{13,9},{6,2},{10,6},{14,10},{7,3},{... | collective-permute-start | bytes 24584 | tf_op jit(solution)/shard_map/ppermute | solution.py:30
  262.6 7.7 %copy-start.25 = (f32[4,168,512]{2,1,0:T(8,128)S(1)}, f32[4,168,512]{2,1,0:T(8,128)}, u32[]{:S(2)}) copy-start(f32[4,168,512]{2,1,0:T(8,128)} %param.13) | copy-start | bytes 4128772
  272.9 1.1 copy-start.7
  275.5 64.2 %reduce-scatter.23.cloned.1.call-start = ((), (), s32[]{:S(2)}) async-start(), calls=%async_computation.15 | async-start | bytes 1310720 | tf_op jit(solution)/shard_map/reduce_scatter | solution.py:86
  276.4 32.3 %collective-permute-start.14 = (f32[4,1,512]{2,1,0:T(1,128)S(1)}, f32[4,1,512]{2,1,0:T(1,128)S(1)}, u32[]{:S(2)}, u32[]{:S(2)}) collective-permute-start(f32[4,1,512]{2,1,0:T(1,128)S(1)} %get-tuple-element.26), channel_id=1, source_target_pairs={{0,4},{4,8},{8,12},{1,5},{5,9},{9,13},{2,6},{6,10},{10,14},{3,7},{... | collective-permute-start | bytes 24584 | tf_op jit(solution)/shard_map/ppermute | solution.py:28
  279.8 28.9 %collective-permute-start.15 = (f32[4,1,512]{2,1,0:T(1,128)S(1)}, f32[4,1,512]{2,1,0:T(1,128)S(1)}, u32[]{:S(2)}, u32[]{:S(2)}) collective-permute-start(f32[4,1,512]{2,1,0:T(1,128)S(1)} %get-tuple-element.27), channel_id=1, source_target_pairs={{4,0},{8,4},{12,8},{5,1},{9,5},{13,9},{6,2},{10,6},{14,10},{7,3},{... | collective-permute-start | bytes 24584 | tf_op jit(solution)/shard_map/ppermute | solution.py:30
  301.0 7.7 %copy-start.8 = (f32[4,168,512]{2,1,0:T(8,128)S(1)}, f32[4,168,512]{2,1,0:T(8,128)}, u32[]{:S(2)}) copy-start(f32[4,168,512]{2,1,0:T(8,128)} %copy-done.7) | copy-start | bytes 4128772
  311.6 1.1 copy-start.12
  312.7 1.5 copy-start.26
  312.7 1.5 copy-start.27
  314.2 25.6 %copy-start.13 = (f32[4,168,64]{1,2,0:T(8,128)S(1)}, f32[4,168,64]{1,2,0:T(8,128)}, u32[]{:S(2)}) copy-start(f32[4,168,64]{1,2,0:T(8,128)} %reduce-scatter.21.cloned.1.call-done) | copy-start | bytes 516100
  327.7 13.7 %copy-start.20 = (f32[4,3,512]{2,0,1:T(4,128)}, f32[4,3,512]{2,0,1:T(4,128)S(1)}, u32[]{:S(2)}) copy-start(f32[4,3,512]{2,0,1:T(4,128)S(1)} %subtract_maximum_fusion) | copy-start | bytes 73732
Sparse Core Ops, SparseCore 0:
  38.0 25.8 reduce-scatter.8
  77.9 25.3 reduce-scatter.10
  117.6 25.3 reduce-scatter.12
  157.6 25.3 reduce-scatter.14
  197.2 25.3 reduce-scatter.16
  237.2 25.3 reduce-scatter.18
  275.6 25.3 reduce-scatter.20
  314.3 25.3 reduce-scatter.22
